TPU v7x, 32 devices: a whole 2x2x4 slice. The times are simulated.
32 devices in a mesh: fsdp: 4 (over y, core), ctx: 2 (over x), tp: 4 (over z).
Axes of the slice: x: 2, y: 2, z: 4, core: 2. Of those that a mesh axis runs over, the one named last changes fastest.
Arguments:
- tokens: bfloat16 [8, 1024, 1024], P('fsdp', 'ctx'), may hold values from -16 to 16
- gain1: bfloat16 [1024], P('fsdp'), may hold values from 0.5 to 1.5
- w_latent: bfloat16 [1024, 512], P('fsdp'), may hold values from -0.1875 to 0.1875
- w_query: bfloat16 [1024, 1024], P('fsdp', 'tp'), may hold values from -0.1875 to 0.1875
- w_key: bfloat16 [256, 1024], P('fsdp', 'tp'), may hold values from -0.375 to 0.375
- w_value: bfloat16 [256, 1024], P('fsdp', 'tp'), may hold values from -0.375 to 0.375
- w_out: bfloat16 [1024, 1024], P('tp', 'fsdp'), may hold values from -1.5 to 1.5
- gain2: bfloat16 [1024], P('fsdp'), may hold values from 0.5 to 1.5
- w_gate: bfloat16 [1024, 2816], P('fsdp', 'tp'), may hold values from -0.1875 to 0.1875
- w_up: bfloat16 [1024, 2816], P('fsdp', 'tp'), may hold values from -0.1875 to 0.1875
- w_down: bfloat16 [2816, 1024], P('tp', 'fsdp'), may hold values from -0.109375 to 0.109375
- segments: int32 [8, 1024], P('fsdp', 'ctx'), may hold values from 0 to 7, never falling along the last dimension, each value on 1 to 512 neighbouring positions
- cotangent: bfloat16 [8, 1024, 1024], P('fsdp', 'ctx'), may hold values from -6 to 6
Outputs:
- mixed: bfloat16 [8, 1024, 1024], P('fsdp', 'ctx')
- grad_tokens: bfloat16 [8, 1024, 1024], P('fsdp', 'ctx')
- grad_gain1: float32 [1024], P('fsdp')
- grad_latent: float32 [1024, 512], P('fsdp')
- grad_query: float32 [1024, 1024], P('fsdp', 'tp')
- grad_key: float32 [256, 1024], P('fsdp', 'tp')
- grad_value: float32 [256, 1024], P('fsdp', 'tp')
- grad_out: float32 [1024, 1024], P('tp', 'fsdp')
- grad_gain2: float32 [1024], P('fsdp')
- grad_gate: float32 [1024, 2816], P('fsdp', 'tp')
- grad_up: float32 [1024, 2816], P('fsdp', 'tp')
- grad_down: float32 [2816, 1024], P('tp', 'fsdp')
- stats: float32 [8, 3], P('fsdp')
- grad_radial: float32 [8, 1024], P('fsdp', 'ctx')
Inputs may be any that keep to these rules, and one draw needn't show every extreme that they name: `segments`: ids never fall along a sequence; every id of 0 to 7 names 1 to 512 consecutive tokens of each sequence, and some id names exactly 512; the largest id of a sequence marks its padding.
All inputs are finite; a program needn't handle non-finite values.
Results may differ from a plain program's by a relative error of at most 0.013.
The roundings to bfloat16 on the way count: a program that leaves them out, or rounds other values in their place, can miss the bound.
Values may be sent and summed in bfloat16 or wider, within the bound.
A program may use at most 128 MiB of HBM per device.

v0:
```python
import jax
import jax.numpy as jnp
from jax import lax
from jax.sharding import PartitionSpec as P

HEADS = 16
HEAD_DIM = 64
GROUPS = 2
LATENT = 256
eps = 1e-05


def precise(left, right):
    return jnp.dot(left, right, precision=lax.Precision.HIGHEST)


def block_scores(query_seq, key_seq, seg_keys, seg_query, q_place, block, tok_dev):
    key_blk = lax.dynamic_slice_in_dim(key_seq, block * tok_dev, tok_dev, 0)
    seg_blk = lax.dynamic_slice_in_dim(seg_keys, block * tok_dev, tok_dev, 0)
    k_place = block * tok_dev + jnp.arange(tok_dev, dtype=jnp.int32)
    counted = (k_place[None, :] <= q_place[:, None]) & (seg_blk[None, :] == seg_query[:, None])
    scores = (
        jnp.einsum("qhd,khd->hqk", query_seq, key_blk, preferred_element_type=jnp.float32) * 0.125
    )
    return (jnp.where(counted[None], scores, -1e30), counted, key_blk)


def norm_back(grad_norm, unit, scale, gain_f):
    scaled = grad_norm * gain_f
    return scale * (scaled - unit * jnp.mean(scaled * unit, axis=-1, keepdims=True))


def on_device(
    tokens,
    gain1,
    w_latent,
    w_query,
    w_key,
    w_value,
    w_out,
    gain2,
    w_gate,
    w_up,
    w_down,
    segments,
    cotangent,
):
    seq_dev, tok_dev, feat_dim = tokens.shape
    n_ctx = lax.axis_size("ctx")
    seq_len = tok_dev * n_ctx
    row_count = seq_dev * tok_dev
    gathered = (
        lax.all_gather(gain1, "fsdp", axis=0, tiled=True),
        lax.all_gather(w_latent, "fsdp", axis=0, tiled=True),
        lax.all_gather(w_query, "fsdp", axis=0, tiled=True),
        lax.all_gather(w_key, "fsdp", axis=0, tiled=True),
        lax.all_gather(w_value, "fsdp", axis=0, tiled=True),
        lax.all_gather(w_out, "fsdp", axis=1, tiled=True),
        lax.all_gather(gain2, "fsdp", axis=0, tiled=True),
        lax.all_gather(w_gate, "fsdp", axis=0, tiled=True),
        lax.all_gather(w_up, "fsdp", axis=0, tiled=True),
        lax.all_gather(w_down, "fsdp", axis=1, tiled=True),
    )
    g_one, w_lat, w_qry, w_kproj, w_vproj, w_outp, g_two, w_gatep, w_upp, w_downp = gathered
    heads_here = w_qry.shape[1] // HEAD_DIM
    q_width = heads_here * HEAD_DIM
    group_at = lax.axis_index("tp") * heads_here // (HEADS // GROUPS)
    lat_cols = lax.dynamic_slice_in_dim(w_lat, group_at * LATENT, LATENT, 1)
    stream = tokens.reshape(row_count, feat_dim).astype(jnp.float32)
    r_one = lax.rsqrt(jnp.mean(stream * stream, axis=-1, keepdims=True) + eps)
    unit_one = stream * r_one
    xn_one = (unit_one * g_one.astype(jnp.float32)).astype(jnp.bfloat16)
    latent = jnp.dot(xn_one, lat_cols, preferred_element_type=jnp.float32).astype(jnp.bfloat16)
    query = jnp.dot(xn_one, w_qry, preferred_element_type=jnp.float32).astype(jnp.bfloat16)
    query = query.reshape(seq_dev, tok_dev, heads_here, HEAD_DIM)
    lat_all, seg_all = (
        lax.all_gather(latent.reshape(seq_dev, tok_dev, LATENT), "ctx", axis=1, tiled=True),
        lax.all_gather(segments.astype(jnp.bfloat16), "ctx", axis=1, tiled=True),
    )
    keys = (
        jnp.dot(lat_all, w_kproj, preferred_element_type=jnp.float32)
        .astype(jnp.bfloat16)
        .reshape(seq_dev, seq_len, heads_here, HEAD_DIM)
    )
    values = (
        jnp.dot(lat_all, w_vproj, preferred_element_type=jnp.float32)
        .astype(jnp.bfloat16)
        .reshape(seq_dev, seq_len, heads_here, HEAD_DIM)
    )
    seg_keys = seg_all.astype(jnp.float32)
    seg_query = segments.astype(jnp.float32)
    ctx_at = lax.axis_index("ctx")
    q_place = ctx_at * tok_dev + jnp.arange(tok_dev, dtype=jnp.int32)
    last_blk = ctx_at + 1
    bounds = []
    lse_list = []
    attn_list = []
    for seq_at in range(seq_dev):
        query_seq = query[seq_at]
        key_seq = keys[seq_at]
        value_seq = values[seq_at]
        seg_k = seg_keys[seq_at]
        seg_q = seg_query[seq_at]
        block_last = seg_k.reshape(n_ctx, tok_dev)[:, -1]
        first_blk = jnp.sum((block_last < seg_q[0]).astype(jnp.int32))
        bounds.append(first_blk)

        def stat_step(block, carry, query_seq=query_seq, key_seq=key_seq, seg_k=seg_k, seg_q=seg_q):
            top, total = carry
            masked, counted, key_blk = block_scores(
                query_seq, key_seq, seg_k, seg_q, q_place, block, tok_dev
            )
            new_top = jnp.maximum(top, jnp.max(masked, axis=-1))
            total = total * jnp.exp(top - new_top) + jnp.sum(
                jnp.where(counted[None], jnp.exp(masked - new_top[..., None]), 0.0), axis=-1
            )
            return (new_top, total)

        start_stats = (
            jnp.full((heads_here, tok_dev), -1e30, jnp.float32),
            jnp.zeros((heads_here, tok_dev), jnp.float32),
        )
        top, total = lax.fori_loop(first_blk, last_blk, stat_step, start_stats)
        lse = top + jnp.log(total)
        lse_list.append(lse)

        def out_step(
            block,
            accum,
            query_seq=query_seq,
            key_seq=key_seq,
            value_seq=value_seq,
            seg_k=seg_k,
            seg_q=seg_q,
            lse=lse,
        ):
            masked, counted, key_blk = block_scores(
                query_seq, key_seq, seg_k, seg_q, q_place, block, tok_dev
            )
            value_blk = lax.dynamic_slice_in_dim(value_seq, block * tok_dev, tok_dev, 0)
            probs = jnp.where(counted[None], jnp.exp(masked - lse[..., None]), 0.0).astype(
                jnp.bfloat16
            )
            return accum + jnp.einsum(
                "hqk,khd->qhd", probs, value_blk, preferred_element_type=jnp.float32
            )

        accum = lax.fori_loop(
            first_blk, last_blk, out_step, jnp.zeros((tok_dev, heads_here, HEAD_DIM), jnp.float32)
        )
        attn_list.append(accum.astype(jnp.bfloat16).reshape(tok_dev, q_width))
    attended = jnp.concatenate(attn_list, axis=0)
    branch = lax.psum(jnp.dot(attended, w_outp, preferred_element_type=jnp.float32), "tp")
    middle = stream + branch
    r_two = lax.rsqrt(jnp.mean(middle * middle, axis=-1, keepdims=True) + eps)
    unit_two = middle * r_two
    xn_two = (unit_two * g_two.astype(jnp.float32)).astype(jnp.bfloat16)
    gate = jnp.dot(xn_two, w_gatep, preferred_element_type=jnp.float32)
    upper = jnp.dot(xn_two, w_upp, preferred_element_type=jnp.float32)
    sigma = jax.nn.sigmoid(gate)
    swish = gate * sigma
    hidden = (swish * upper).astype(jnp.bfloat16)
    feed = lax.psum(
        jnp.dot(hidden, w_downp, preferred_element_type=jnp.float32).astype(jnp.bfloat16), "tp"
    ).astype(jnp.float32)
    mixed = middle + feed
    valid = (seg_query != seg_keys[:, -1:]).astype(jnp.float32)
    valid_three = valid[:, :, None]

    def seq_squares(field):
        shaped = field.reshape(seq_dev, tok_dev, feat_dim)
        return jnp.sum(valid_three * shaped * shaped, axis=(1, 2))

    squares = jnp.stack([seq_squares(mixed), seq_squares(branch), seq_squares(feed)], axis=1)
    squares, counted_rows = lax.psum((squares, jnp.sum(valid, axis=1)), "ctx")
    stats = jnp.sqrt(squares / (counted_rows[:, None] * feat_dim))
    b_gone, b_lat, b_qry, b_kproj, b_vproj, b_outp, b_gtwo, b_gatep, b_upp, b_downp = gathered
    b_latcols = lax.dynamic_slice_in_dim(b_lat, group_at * LATENT, LATENT, 1)
    out_grad = cotangent.reshape(row_count, feat_dim)
    grad_down = jnp.dot(hidden.T, out_grad, preferred_element_type=jnp.float32)
    d_hidden = jnp.dot(out_grad, b_downp.T, preferred_element_type=jnp.float32)
    d_gate = (d_hidden * upper * sigma * (1.0 + gate * (1.0 - sigma))).astype(jnp.bfloat16)
    d_upper = (d_hidden * swish).astype(jnp.bfloat16)
    grad_gate = jnp.dot(xn_two.T, d_gate, preferred_element_type=jnp.float32)
    grad_up = jnp.dot(xn_two.T, d_upper, preferred_element_type=jnp.float32)
    part_two = jnp.dot(d_gate, b_gatep.T, preferred_element_type=jnp.float32) + jnp.dot(
        d_upper, b_upp.T, preferred_element_type=jnp.float32
    )
    d_xntwo = lax.psum(part_two, "tp")
    grad_gtwo = jnp.sum(d_xntwo * unit_two, axis=0)
    d_middle = out_grad.astype(jnp.float32) + norm_back(
        d_xntwo, unit_two, r_two, b_gtwo.astype(jnp.float32)
    )
    d_branch = d_middle.astype(jnp.bfloat16)
    grad_outp = jnp.dot(attended.T, d_branch, preferred_element_type=jnp.float32)
    d_attn = jnp.dot(d_branch, b_outp.T, preferred_element_type=jnp.float32).astype(jnp.bfloat16)
    d_attn = d_attn.reshape(seq_dev, tok_dev, heads_here, HEAD_DIM)
    dq_list = []
    dk_list = []
    dv_list = []
    for seq_at in range(seq_dev):
        query_seq = query[seq_at]
        key_seq = keys[seq_at]
        value_seq = values[seq_at]
        seg_k = seg_keys[seq_at]
        seg_q = seg_query[seq_at]
        lse = lse_list[seq_at]
        grad_seq = d_attn[seq_at]
        first_blk = bounds[seq_at]

        def delta_step(
            block,
            delta,
            query_seq=query_seq,
            key_seq=key_seq,
            value_seq=value_seq,
            seg_k=seg_k,
            seg_q=seg_q,
            lse=lse,
            grad_seq=grad_seq,
        ):
            masked, counted, key_blk = block_scores(
                query_seq, key_seq, seg_k, seg_q, q_place, block, tok_dev
            )
            value_blk = lax.dynamic_slice_in_dim(value_seq, block * tok_dev, tok_dev, 0)
            probs = jnp.where(counted[None], jnp.exp(masked - lse[..., None]), 0.0)
            d_prob = jnp.einsum(
                "qhd,khd->hqk", grad_seq, value_blk, preferred_element_type=jnp.float32
            )
            return delta + jnp.sum(probs * d_prob, axis=-1)

        delta = lax.fori_loop(
            first_blk, last_blk, delta_step, jnp.zeros((heads_here, tok_dev), jnp.float32)
        )

        def grad_step(
            block,
            carry,
            query_seq=query_seq,
            key_seq=key_seq,
            value_seq=value_seq,
            seg_k=seg_k,
            seg_q=seg_q,
            lse=lse,
            grad_seq=grad_seq,
            delta=delta,
        ):
            d_query, d_keys, d_values = carry
            masked, counted, key_blk = block_scores(
                query_seq, key_seq, seg_k, seg_q, q_place, block, tok_dev
            )
            value_blk = lax.dynamic_slice_in_dim(value_seq, block * tok_dev, tok_dev, 0)
            probs = jnp.where(counted[None], jnp.exp(masked - lse[..., None]), 0.0)
            d_prob = jnp.einsum(
                "qhd,khd->hqk", grad_seq, value_blk, preferred_element_type=jnp.float32
            )
            d_score = (probs * (d_prob - delta[..., None])).astype(jnp.bfloat16)
            d_query = d_query + 0.125 * jnp.einsum(
                "hqk,khd->qhd", d_score, key_blk, preferred_element_type=jnp.float32
            )
            d_keyblk = 0.125 * jnp.einsum(
                "hqk,qhd->khd", d_score, query_seq, preferred_element_type=jnp.float32
            )
            d_valblk = jnp.einsum(
                "hqk,qhd->khd",
                probs.astype(jnp.bfloat16),
                grad_seq,
                preferred_element_type=jnp.float32,
            )
            d_keys = lax.dynamic_update_slice_in_dim(d_keys, d_keyblk, block * tok_dev, 0)
            d_values = lax.dynamic_update_slice_in_dim(d_values, d_valblk, block * tok_dev, 0)
            return (d_query, d_keys, d_values)

        zero_keys = jnp.zeros((seq_len, heads_here, HEAD_DIM), jnp.float32)
        start_grads = (
            jnp.zeros((tok_dev, heads_here, HEAD_DIM), jnp.float32),
            zero_keys,
            zero_keys,
        )
        d_query, d_keys, d_values = lax.fori_loop(first_blk, last_blk, grad_step, start_grads)
        dq_list.append(d_query.astype(jnp.bfloat16).reshape(tok_dev, q_width))
        dk_list.append(d_keys.reshape(seq_len, q_width))
        dv_list.append(d_values.reshape(seq_len, q_width))
    d_query = jnp.concatenate(dq_list, axis=0)
    d_keys = jnp.stack(dk_list, axis=0)
    d_values = jnp.stack(dv_list, axis=0)
    own_keys, own_values = (
        lax.psum_scatter(d_keys, "ctx", scatter_dimension=1, tiled=True),
        lax.psum_scatter(d_values, "ctx", scatter_dimension=1, tiled=True),
    )
    own_keys = own_keys.reshape(row_count, q_width).astype(jnp.bfloat16)
    own_values = own_values.reshape(row_count, q_width).astype(jnp.bfloat16)
    grad_kproj = jnp.dot(latent.T, own_keys, preferred_element_type=jnp.float32)
    grad_vproj = jnp.dot(latent.T, own_values, preferred_element_type=jnp.float32)
    d_latent = jnp.dot(own_keys, b_kproj.T, preferred_element_type=jnp.float32) + jnp.dot(
        own_values, b_vproj.T, preferred_element_type=jnp.float32
    )
    grad_qry = jnp.dot(xn_one.T, d_query, preferred_element_type=jnp.float32)
    grad_latcols = precise(xn_one.astype(jnp.float32).T, d_latent)
    grad_lat = lax.dynamic_update_slice_in_dim(
        jnp.zeros((feat_dim, GROUPS * LATENT), jnp.float32), grad_latcols, group_at * LATENT, 1
    )
    part_one = jnp.dot(d_query, b_qry.T, preferred_element_type=jnp.float32) + precise(
        d_latent, b_latcols.astype(jnp.float32).T
    )
    d_xnone = lax.psum(part_one, "tp")
    grad_gone = jnp.sum(d_xnone * unit_one, axis=0)
    d_stream = d_middle + norm_back(d_xnone, unit_one, r_one, b_gone.astype(jnp.float32))
    radial = (jnp.sum(unit_one * d_stream, axis=-1) / jnp.sqrt(jnp.float32(feat_dim))).reshape(
        seq_dev, tok_dev
    )
    shards = (
        lax.psum_scatter(grad_gone, "fsdp", scatter_dimension=0, tiled=True),
        lax.psum_scatter(grad_lat, "fsdp", scatter_dimension=0, tiled=True),
        lax.psum_scatter(grad_qry, "fsdp", scatter_dimension=0, tiled=True),
        lax.psum_scatter(grad_kproj, "fsdp", scatter_dimension=0, tiled=True),
        lax.psum_scatter(grad_vproj, "fsdp", scatter_dimension=0, tiled=True),
        lax.psum_scatter(grad_outp, "fsdp", scatter_dimension=1, tiled=True),
        lax.psum_scatter(grad_gtwo, "fsdp", scatter_dimension=0, tiled=True),
        lax.psum_scatter(grad_gate, "fsdp", scatter_dimension=0, tiled=True),
        lax.psum_scatter(grad_up, "fsdp", scatter_dimension=0, tiled=True),
        lax.psum_scatter(grad_down, "fsdp", scatter_dimension=1, tiled=True),
    )
    s_gone, s_lat, s_qry, s_kproj, s_vproj, s_outp, s_gtwo, s_gate, s_upp, s_down = shards
    summed = lax.psum(
        (s_gone, s_qry, s_kproj, s_vproj, s_outp, s_gtwo, s_gate, s_upp, s_down), "ctx"
    )
    s_lat = lax.psum(s_lat, ("ctx", "tp"))
    f_gone, f_qry, f_kproj, f_vproj, f_outp, f_gtwo, f_gate, f_upp, f_down = summed
    mixed_out = mixed.reshape(seq_dev, tok_dev, feat_dim).astype(jnp.bfloat16)
    grad_tokens = d_stream.reshape(seq_dev, tok_dev, feat_dim).astype(jnp.bfloat16)
    return (
        mixed_out,
        grad_tokens,
        f_gone,
        s_lat,
        f_qry,
        f_kproj,
        f_vproj,
        f_outp,
        f_gtwo,
        f_gate,
        f_upp,
        f_down,
        stats,
        radial,
    )


def solution(mesh):
    return jax.shard_map(
        on_device,
        mesh=mesh,
        in_specs=(
            P("fsdp", "ctx", None),
            P("fsdp"),
            P("fsdp", None),
            P("fsdp", "tp"),
            P("fsdp", "tp"),
            P("fsdp", "tp"),
            P("tp", "fsdp"),
            P("fsdp"),
            P("fsdp", "tp"),
            P("fsdp", "tp"),
            P("tp", "fsdp"),
            P("fsdp", "ctx"),
            P("fsdp", "ctx", None),
        ),
        out_specs=(
            P("fsdp", "ctx", None),
            P("fsdp", "ctx", None),
            P("fsdp"),
            P("fsdp", None),
            P("fsdp", "tp"),
            P("fsdp", "tp"),
            P("fsdp", "tp"),
            P("tp", "fsdp"),
            P("fsdp"),
            P("fsdp", "tp"),
            P("fsdp", "tp"),
            P("tp", "fsdp"),
            P("fsdp", None),
            P("fsdp", "ctx"),
        ),
        check_vma=False,
    )
```

profile of v0, /device:TPU:0, one launch (start us, length us, event | category | flops | bytes accessed | tf_op | source)
XLA Modules:
  0.0 1288.4 jit_solution(14811559421376476977)
XLA Ops:
  8.0 2.1 fusion.143
  10.8 6.0 all-gather
  17.5 4.3 all_gather.36
  25.2 7.9 all_gather.42
  33.1 7.5 all_gather.43
  42.4 3.3 convolution_convert_fusion.5
  45.9 5.4 all_gather.41
  53.9 5.4 all_gather.40
  60.2 7.7 all-gather.10.cloned.1.call-done
  69.7 2.4 while.100
  73.7 3.2 while.101
  74.1 2.8 fusion.301
  76.9 2.4 while.102
  79.4 3.4 while.103
  80.0 2.7 fusion.307
  82.9 2.7 fusion.153
  87.4 5.1 all-gather.1
  92.5 158.9 %all-reduce.12.cloned.1.call-done = f32[1024,1024]{1,0:T(8,128)} async-done(((f32[1024,1024]{1,0:T(8,128)}), f32[1024,1024]{1,0:T(8,128)}) %all-reduce.12.cloned.1.call-update) | async-done | bytes 4194320 | tf_op jit(solution)/shard_map/psum | solution.py:153
  251.4 3.5 multiply_reduce_fusion.2
  258.6 12.4 all-gather.12.cloned.1.call-done
  271.0 5.3 fusion.175
  276.3 15.3 %all-gather.14.cloned.1.call-done = bf16[1024,704]{0,1:T(8,128)(2,1)} async-done(((bf16[256,704]{0,1:T(8,128)(2,1)}), bf16[1024,704]{0,1:T(8,128)(2,1)}) %all-gather.14.cloned.1.call-update) | async-done | bytes 1441808 | tf_op jit(solution)/shard_map/all_gather | solution.py:61
  291.6 5.3 fusion.176
  296.9 15.3 %all-gather.16.cloned.1.call-done = bf16[704,1024]{1,0:T(8,128)(2,1)} async-done(((bf16[704,256]{1,0:T(8,128)(2,1)}), bf16[704,1024]{1,0:T(8,128)(2,1)}) %all-gather.16.cloned.1.call-update) | async-done | bytes 1441808 | tf_op jit(solution)/shard_map/all_gather | solution.py:62
  312.2 8.2 multiply_convert_fusion.1
  321.5 3.2 convolution_convert_fusion
  325.2 3.8 fusion.177
  329.0 3.9 convolution_add_fusion.1
  335.2 76.2 %all-reduce.14.cloned.1.call-done = bf16[1024,1024]{1,0:T(8,128)(2,1)} async-done(((bf16[1024,1024]{1,0:T(8,128)(2,1)}), bf16[1024,1024]{1,0:T(8,128)(2,1)}) %all-reduce.14.cloned.1.call-update) | async-done | bytes 2097168 | tf_op jit(solution)/shard_map/psum | solution.py:163
  411.4 156.3 %all-reduce.16.cloned.1.call-done = f32[1024,1024]{1,0:T(8,128)} async-done(((f32[1024,1024]{1,0:T(8,128)}), f32[1024,1024]{1,0:T(8,128)}) %all-reduce.16.cloned.1.call-update) | async-done | bytes 4194320 | tf_op jit(solution)/shard_map/psum | solution.py:189
  567.7 8.5 fusion.129
  581.3 2.8 while.104
  586.1 9.7 while.105
  591.6 2.3 fusion.328
  595.8 2.8 while.106
  600.9 10.0 while.107
  606.8 2.3 fusion.349
  610.9 3.1 pad_maximum_fusion.1
  614.1 2.8 pad_maximum_fusion
  617.2 5.4 fusion.182
  622.7 4.8 fusion.183
  627.6 5.3 fusion.181
  633.0 3.3 fusion.151
  636.4 4.0 fusion.146
  640.5 2.9 fusion.152
  643.4 25.1 %reduce-scatter.13.cloned.1.call-done = f32[2,512,256]{1,2,0:T(8,128)} async-done(((f32[2,1024,256]{1,2,0:T(8,128)}), f32[2,512,256]{1,2,0:T(8,128)}) %reduce-scatter.13.cloned.1.call-update) | async-done | bytes 1048592 | tf_op jit(solution)/shard_map/reduce_scatter | solution.py:289
  670.0 32.4 %reduce-scatter.11.cloned.1.call-done = f32[2,512,256]{1,2,0:T(8,128)} async-done(((f32[2,1024,256]{1,2,0:T(8,128)}), f32[2,512,256]{1,2,0:T(8,128)}) %reduce-scatter.11.cloned.1.call-update) | async-done | bytes 1048592 | tf_op jit(solution)/shard_map/reduce_scatter | solution.py:288
  707.9 6.2 convolution_add_fusion
  716.2 5.5 convolution_dynamic-update-slice_fusion
  721.7 19.8 %reduce-scatter.25.cloned.1.call-done = f32[256,704]{0,1:T(8,128)} async-done(((f32[1024,704]{0,1:T(8,128)}), f32[256,704]{0,1:T(8,128)}) %reduce-scatter.25.cloned.1.call-update) | async-done | bytes 720912 | tf_op jit(solution)/shard_map/reduce_scatter | solution.py:320
  741.6 38.8 %reduce-scatter.27.cloned.1.call-done = f32[256,704]{0,1:T(8,128)} async-done(((f32[1024,704]{0,1:T(8,128)}), f32[256,704]{0,1:T(8,128)}) %reduce-scatter.27.cloned.1.call-update) | async-done | bytes 720912 | tf_op jit(solution)/shard_map/reduce_scatter | solution.py:321
  780.3 39.1 %reduce-scatter.29.cloned.1.call-done = f32[704,256]{1,0:T(8,128)} async-done(((f32[704,1024]{1,0:T(8,128)}), f32[704,256]{1,0:T(8,128)}) %reduce-scatter.29.cloned.1.call-update) | async-done | bytes 720912 | tf_op jit(solution)/shard_map/reduce_scatter | solution.py:322
  819.4 27.3 %reduce-scatter.17.cloned.1.call-done = f32[256,256]{1,0:T(8,128)} async-done(((f32[1024,256]{1,0:T(8,128)}), f32[256,256]{1,0:T(8,128)}) %reduce-scatter.17.cloned.1.call-update) | async-done | bytes 262160 | tf_op jit(solution)/shard_map/reduce_scatter | solution.py:315
  846.7 27.4 %reduce-scatter.23.cloned.1.call-done = f32[256,256]{1,0:T(8,128)} async-done(((f32[256,1024]{1,0:T(8,128)}), f32[256,256]{1,0:T(8,128)}) %reduce-scatter.23.cloned.1.call-update) | async-done | bytes 262160 | tf_op jit(solution)/shard_map/reduce_scatter | solution.py:318
  874.2 23.0 %reduce-scatter.21.cloned.1.call-done = f32[64,256]{1,0:T(8,128)} async-done(((f32[256,256]{1,0:T(8,128)}), f32[64,256]{1,0:T(8,128)}) %reduce-scatter.21.cloned.1.call-update) | async-done | bytes 65552 | tf_op jit(solution)/shard_map/reduce_scatter | solution.py:317
  897.1 23.1 %reduce-scatter.19.cloned.1.call-done = f32[64,256]{1,0:T(8,128)} async-done(((f32[256,256]{1,0:T(8,128)}), f32[64,256]{1,0:T(8,128)}) %reduce-scatter.19.cloned.1.call-update) | async-done | bytes 65552 | tf_op jit(solution)/shard_map/reduce_scatter | solution.py:316
  922.2 155.3 %all-reduce.18.cloned.1.call-done = f32[1024,1024]{1,0:T(8,128)} async-done(((f32[1024,1024]{1,0:T(8,128)}), f32[1024,1024]{1,0:T(8,128)}) %all-reduce.18.cloned.1.call-update) | async-done | bytes 4194320 | tf_op jit(solution)/shard_map/psum | solution.py:306
  1077.5 3.2 fusion.137
  1080.9 4.8 fusion.142
  1085.7 7.0 all-reduce.2
  1092.9 5.5 all-reduce.3
  1098.4 12.2 reduce-scatter.15.cloned.1.call-done
  1112.0 81.0 %all-reduce.22.cloned.1.call-done = (f32[256,256]{1,0:T(8,128)}, f32[64,256]{1,0:T(8,128)}, f32[64,256]{1,0:T(8,128)}, f32[256,256]{1,0:T(8,128)}, f32[256,704]{...) async-done(((f32[256,256]{1,0:T(8,128)}, f32[64,256]{1,0:T(8,128)}, f32[64,256]{1,0:T(8,128)}, f32[256,256]{1,0:T(8,128)}, f32[256,704]{0,1:T(8,128)}, ...) | async-done | bytes 2818064 | tf_op jit(solution)/shard_map/psum | solution.py:325
  1193.0 76.2 %all-reduce.20.cloned.1.call-done = f32[256,512]{1,0:T(8,128)} async-done(((f32[256,512]{1,0:T(8,128)}), f32[256,512]{1,0:T(8,128)}) %all-reduce.20.cloned.1.call-update) | async-done | bytes 524304 | tf_op jit(solution)/shard_map/psum | solution.py:328
  (285 shorter events, 73.0 us)
Async XLA Ops:
  7.2 33.4 %copy-start.4 = (bf16[2,512,1024]{2,1,0:T(8,128)(2,1)S(1)}, bf16[2,512,1024]{2,1,0:T(8,128)(2,1)}, u32[]{:S(2)}) copy-start(bf16[2,512,1024]{2,1,0:T(8,128)(2,1)} %param.29) | copy-start | bytes 6291460
  7.2 35.3 %all-gather.8.cloned.1.call-start = ((), (), s32[]{:S(2)}) async-start(), calls=%async_computation.10 | async-start | bytes 1310720 | tf_op jit(solution)/shard_map/all_gather | solution.py:54
  7.9 59.9 %all-gather.10.cloned.1.call-start = ((), (), s32[]{:S(2)}) async-start(), calls=%async_computation.11 | async-start | bytes 1572864 | tf_op jit(solution)/shard_map/all_gather | solution.py:77
  10.1 35.7 %copy-start.32 = (f32[1,4,2,128]{3,1,2,0:T(4,128)}, f32[1,4,2,128]{3,1,2,0:T(4,128)S(1)}, u32[]{:S(2)}) copy-start(f32[1,4,2,128]{3,1,2,0:T(4,128)S(1)} %copy.94) | copy-start | bytes 12292
  16.8 29.0 %copy-start.34 = (f32[4,1,256]{2,1,0:T(1,128)}, f32[4,1,256]{2,1,0:T(1,128)S(1)}, u32[]{:S(2)}) copy-start(f32[4,1,256]{2,1,0:T(1,128)S(1)} %convert_element_type.173) | copy-start | bytes 12292
  21.9 18.7 %copy-start.40 = (f32[2,1024]{1,0:T(2,128)}, f32[2,1024]{1,0:T(2,128)S(1)}, u32[]{:S(2)}) copy-start(f32[2,1024]{1,0:T(2,128)S(1)} %convert_element_type.138) | copy-start | bytes 24580
  33.1 26.3 %copy-start.17 = (bf16[1024,256]{1,0:T(8,128)(2,1)}, bf16[1024,256]{1,0:T(8,128)(2,1)S(1)}, u32[]{:S(2)}) copy-start(bf16[1024,256]{1,0:T(8,128)(2,1)S(1)} %all_gather.42) | copy-start | bytes 1572868
  42.4 3.4 copy-start.38
  42.4 11.4 copy-start.39
  42.4 16.9 %copy-start.8 = (bf16[1024,1024]{1,0:T(8,128)(2,1)S(1)}, bf16[1024,1024]{1,0:T(8,128)(2,1)}, u32[]{:S(2)}) copy-start(bf16[1024,1024]{1,0:T(8,128)(2,1)} %fusion.136) | copy-start | bytes 6291460
  45.8 205.6 %all-reduce.12.cloned.1.call-start = ((), (), s32[]{:S(2)}) async-start(), calls=%async_computation.12 | async-start | bytes 8388608 | tf_op jit(solution)/shard_map/psum | solution.py:153
  51.3 16.6 %copy-start.20 = (bf16[256,256]{1,0:T(8,128)(2,1)}, bf16[256,256]{1,0:T(8,128)(2,1)S(1)}, u32[]{:S(2)}) copy-start(bf16[256,256]{1,0:T(8,128)(2,1)S(1)} %all_gather.41) | copy-start | bytes 393220
  59.3 12.8 copy-start.22
  69.7 2.4 copy-start.10
  76.9 5.9 copy-start.13
  82.8 2.8 copy-start.15
  85.6 185.4 %all-gather.12.cloned.1.call-start = ((), (), s32[]{:S(2)}) async-start(), calls=%async_computation.13 | async-start | bytes 1802240 | tf_op jit(solution)/shard_map/all_gather | solution.py:60
  86.2 205.4 %all-gather.14.cloned.1.call-start = ((), (), s32[]{:S(2)}) async-start(), calls=%async_computation.14 | async-start | bytes 1802240 | tf_op jit(solution)/shard_map/all_gather | solution.py:61
  86.8 225.4 %all-gather.16.cloned.1.call-start = ((), (), s32[]{:S(2)}) async-start(), calls=%async_computation.15 | async-start | bytes 1802240 | tf_op jit(solution)/shard_map/all_gather | solution.py:62
  87.4 324.0 %all-reduce.14.cloned.1.call-start = ((), (), s32[]{:S(2)}) async-start(), calls=%async_computation.16 | async-start | bytes 4194304 | tf_op jit(solution)/shard_map/psum | solution.py:163
  254.9 2.0 copy-start.2
  312.2 9.3 copy-start.48
  324.7 243.0 %all-reduce.16.cloned.1.call-start = ((), (), s32[]{:S(2)}) async-start(), calls=%async_computation.17 | async-start | bytes 8388608 | tf_op jit(solution)/shard_map/psum | solution.py:189
  325.2 3.8 copy-start.47
  325.2 3.8 copy-start.51
  332.9 2.2 copy-start.36
  332.9 335.6 %reduce-scatter.13.cloned.1.call-start = ((), (), s32[]{:S(2)}) async-start(), calls=%async_computation.19 | async-start | bytes 3145728 | tf_op jit(solution)/shard_map/reduce_scatter | solution.py:289
  335.1 241.1 %copy-start.45 = (f32[2]{0:T(128)}, f32[2]{0:T(128)S(1)}, u32[]{:S(2)}) copy-start(f32[2]{0:T(128)S(1)} %slice_reduce_fusion) | copy-start | bytes 28
  567.7 8.5 copy-start.3
  567.7 8.5 copy-start.6
  567.7 9.1 copy-start.19
  578.3 1.9 copy-start
  614.1 88.4 %reduce-scatter.11.cloned.1.call-start = ((), (), s32[]{:S(2)}) async-start(), calls=%async_computation.18 | async-start | bytes 3145728 | tf_op jit(solution)/shard_map/reduce_scatter | solution.py:288
  616.9 5.7 copy-start.52
  617.0 124.6 %reduce-scatter.25.cloned.1.call-start = ((), (), s32[]{:S(2)}) async-start(), calls=%async_computation.27 | async-start | bytes 3604480 | tf_op jit(solution)/shard_map/reduce_scatter | solution.py:320
  622.6 157.7 %reduce-scatter.27.cloned.1.call-start = ((), (), s32[]{:S(2)}) async-start(), calls=%async_computation.28 | async-start | bytes 3604480 | tf_op jit(solution)/shard_map/reduce_scatter | solution.py:321
  627.5 191.9 %reduce-scatter.29.cloned.1.call-start = ((), (), s32[]{:S(2)}) async-start(), calls=%async_computation.29 | async-start | bytes 3604480 | tf_op jit(solution)/shard_map/reduce_scatter | solution.py:322
  632.8 3.6 copy-start.14
  632.8 3.6 copy-start.16
  632.9 213.9 %reduce-scatter.17.cloned.1.call-start = ((), (), s32[]{:S(2)}) async-start(), calls=%async_computation.23 | async-start | bytes 1310720 | tf_op jit(solution)/shard_map/reduce_scatter | solution.py:315
  636.3 4.2 copy-start.18
  636.3 237.8 %reduce-scatter.23.cloned.1.call-start = ((), (), s32[]{:S(2)}) async-start(), calls=%async_computation.26 | async-start | bytes 1310720 | tf_op jit(solution)/shard_map/reduce_scatter | solution.py:318
  640.5 63.5 %copy-start.9 = (bf16[1024,256]{1,0:T(8,128)(2,1)S(1)}, bf16[1024,256]{1,0:T(8,128)(2,1)}, u32[]{:S(2)}) copy-start(bf16[1024,256]{1,0:T(8,128)(2,1)} %convolution_convert_fusion.5) | copy-start | bytes 1572868
  640.5 256.7 %reduce-scatter.21.cloned.1.call-start = ((), (), s32[]{:S(2)}) async-start(), calls=%async_computation.25 | async-start | bytes 327680 | tf_op jit(solution)/shard_map/reduce_scatter | solution.py:317
  643.4 62.8 %copy-start.21 = (bf16[256,256]{1,0:T(8,128)(2,1)S(1)}, bf16[256,256]{1,0:T(8,128)(2,1)}, u32[]{:S(2)}) copy-start(bf16[256,256]{1,0:T(8,128)(2,1)} %copy-done.20) | copy-start | bytes 393220
  669.8 36.7 %copy-start.23 = (bf16[256,256]{1,0:T(8,128)(2,1)S(1)}, bf16[256,256]{1,0:T(8,128)(2,1)}, u32[]{:S(2)}) copy-start(bf16[256,256]{1,0:T(8,128)(2,1)} %copy-done.22) | copy-start | bytes 393220
  705.1 215.2 %reduce-scatter.19.cloned.1.call-start = ((), (), s32[]{:S(2)}) async-start(), calls=%async_computation.24 | async-start | bytes 327680 | tf_op jit(solution)/shard_map/reduce_scatter | solution.py:316
  706.5 371.0 %all-reduce.18.cloned.1.call-start = ((), (), s32[]{:S(2)}) async-start(), calls=%async_computation.20 | async-start | bytes 8388608 | tf_op jit(solution)/shard_map/psum | solution.py:306
  714.2 396.5 %reduce-scatter.15.cloned.1.call-start = ((), (), s32[]{:S(2)}) async-start(), calls=%async_computation.21 | async-start | bytes 2621440 | tf_op jit(solution)/shard_map/reduce_scatter | solution.py:314
  716.1 204.2 %copy-start.50 = (u32[32]{0:T(128)S(1)}, u32[32]{0:T(128)}, u32[]{:S(2)}) copy-start(u32[32]{0:T(128)} %constant.179) | copy-start | bytes 388
  716.1 205.4 %copy-start.37 = (s32[2,512]{1,0:T(2,128)S(1)}, s32[2,512]{1,0:T(2,128)}, u32[]{:S(2)}) copy-start(s32[2,512]{1,0:T(2,128)} %param.40) | copy-start | bytes 12292
  716.1 205.4 %copy-start.46 = (f32[2]{0:T(128)S(1)}, f32[2]{0:T(128)}, u32[]{:S(2)}) copy-start(f32[2]{0:T(128)} %copy-done.45) | copy-start | bytes 28
  716.1 205.6 %copy-start.44 = (f32[1024]{0:T(1024)S(1)}, f32[1024]{0:T(1024)}, u32[]{:S(2)}) copy-start(f32[1024]{0:T(1024)} %get-tuple-element.1042) | copy-start | bytes 12292
  716.1 205.6 %copy-start.43 = (f32[1024]{0:T(1024)S(1)}, f32[1024]{0:T(1024)}, u32[]{:S(2)}) copy-start(f32[1024]{0:T(1024)} %get-tuple-element.823) | copy-start | bytes 12292
  716.1 205.7 %copy-start.42 = (f32[1024]{0:T(1024)S(1)}, f32[1024]{0:T(1024)}, u32[]{:S(2)}) copy-start(f32[1024]{0:T(1024)} %get-tuple-element.824) | copy-start | bytes 12292
  716.2 361.3 %copy-start.5 = (bf16[2,512,1024]{2,1,0:T(8,128)(2,1)S(1)}, bf16[2,512,1024]{2,1,0:T(8,128)(2,1)}, u32[]{:S(2)}) copy-start(bf16[2,512,1024]{2,1,0:T(8,128)(2,1)} %param.29) | copy-start | bytes 6291460
  716.2 361.3 %copy-start.33 = (f32[1,4,2,128]{3,1,2,0:T(4,128)S(1)}, f32[1,4,2,128]{3,1,2,0:T(4,128)}, u32[]{:S(2)}) copy-start(f32[1,4,2,128]{3,1,2,0:T(4,128)} %copy-done.32) | copy-start | bytes 12292
  716.2 361.3 %copy-start.35 = (f32[4,1,256]{2,1,0:T(1,128)S(1)}, f32[4,1,256]{2,1,0:T(1,128)}, u32[]{:S(2)}) copy-start(f32[4,1,256]{2,1,0:T(1,128)} %copy-done.34) | copy-start | bytes 12292
  721.7 471.3 %all-reduce.22.cloned.1.call-start = ((), (), s32[]{:S(2)}) async-start(), calls=%async_computation.30 | async-start | bytes 5636096 | tf_op jit(solution)/shard_map/psum | solution.py:325
  920.3 348.9 %all-reduce.20.cloned.1.call-start = ((), (), s32[]{:S(2)}) async-start(), calls=%async_computation.22 | async-start | bytes 1048576 | tf_op jit(solution)/shard_map/psum | solution.py:328
  1077.5 3.5 copy-start.1
  1080.9 4.8 copy-start.41
  1193.0 86.4 %copy-start.25 = (f32[256,704]{0,1:T(8,128)S(1)}, f32[256,704]{0,1:T(8,128)}, u32[]{:S(2)}) copy-start(f32[256,704]{0,1:T(8,128)} %get-tuple-element.2015) | copy-start | bytes 2162692
  1193.0 87.2 %copy-start.24 = (f32[704,256]{1,0:T(8,128)S(1)}, f32[704,256]{1,0:T(8,128)}, u32[]{:S(2)}) copy-start(f32[704,256]{1,0:T(8,128)} %get-tuple-element.2016) | copy-start | bytes 2162692
  (11 other events, 13.0 us)
Sparse Core Ops, SparseCore 0:
  9.6 19.4 all-gather.7
  45.9 21.8 all-gather.9
  85.7 165.5 all-reduce.11
  252.9 18.0 all-gather.11
  272.5 19.0 all-gather.13
  293.1 19.0 all-gather.15
  324.8 86.4 all-reduce.13
  413.7 153.9 all-reduce.15
  614.2 54.2 reduce-scatter.12
  670.6 31.8 reduce-scatter.10
  705.2 36.3 reduce-scatter.24
  744.0 36.3 reduce-scatter.26
  783.0 36.3 reduce-scatter.28
  821.8 24.8 reduce-scatter.16
  849.3 24.8 reduce-scatter.22
  877.1 20.0 reduce-scatter.20
  900.2 20.0 reduce-scatter.18
  922.4 154.9 all-reduce.17
  1080.2 30.4 reduce-scatter.14
  1113.2 79.7 all-reduce.21
  1196.8 72.3 all-reduce.19
where the time goes:
time: 1300 us; the launch traced here: 1290 us
  waiting for transfers between devices  1030 us (79%)
  matrix products  104 us (8%)
  blocking collectives  54.2 us (4%)
  other arithmetic  44.3 us (3%)
  local copies, waits for them, and re-layouts  32 us (2%)
  between operations  20.1 us (2%)
    psum x1, waiting for transfers between devices, on_device(): lax.psum(jnp.dot(attended, w_outp, preferred_element_type=jnp.float32), '...  159 us
    psum x1, waiting for transfers between devices, on_device(): d_xntwo = lax.psum(part_two, 'tp')  156 us
    psum x1, waiting for transfers between devices, on_device(): d_xnone = lax.psum(part_one, 'tp')  155 us
    psum x1, waiting for transfers between devices, on_device(): lax.psum((s_gone, s_qry, s_kproj, s_vproj, s_outp, s_gtwo, s_gate, s_upp,...  81 us
    psum x1, waiting for transfers between devices, on_device(): s_lat = lax.psum(s_lat, ('ctx', 'tp'))  76.2 us
    psum x1, waiting for transfers between devices, on_device(): lax.psum(jnp.dot(hidden, w_downp, preferred_element_type=jnp.float32).ast...  76.2 us
    reduce_scatter x1, waiting for transfers between devices, on_device(): lax.psum_scatter(grad_down, 'fsdp', scatter_dimension=1, tiled=True)  39.1 us
    reduce_scatter x1, waiting for transfers between devices, on_device(): lax.psum_scatter(grad_up, 'fsdp', scatter_dimension=0, tiled=True)  38.8 us
  transfers between devices with their start and end apart: 21, of which 20 were waited for; matrix products, arithmetic and copies ran while one was open for 7% of the time, Pallas kernels for 0%

commit v1 on v0

--- a/solution.py
+++ b/solution.py
@@ -325,7 +325,7 @@
     summed = lax.psum(
         (s_gone, s_qry, s_kproj, s_vproj, s_outp, s_gtwo, s_gate, s_upp, s_down), "ctx"
     )
-    s_lat = lax.psum(s_lat, ("ctx", "tp"))
+    s_lat = lax.psum(lax.psum(s_lat, "tp"), "ctx")
     f_gone, f_qry, f_kproj, f_vproj, f_outp, f_gtwo, f_gate, f_upp, f_down = summed
     mixed_out = mixed.reshape(seq_dev, tok_dev, feat_dim).astype(jnp.bfloat16)
     grad_tokens = d_stream.reshape(seq_dev, tok_dev, feat_dim).astype(jnp.bfloat16)

time: 1300 us -> 1260 us (0.969)
  waiting for transfers between devices: 1030 us -> 988 us
    psum x2 -> x1, waiting for transfers between devices: 157 us -> 68.8 us  [on_device(): s_lat = lax.psum(lax.psum(s_lat, 'tp'), 'ctx')]
    reduce_scatter x1, waiting for transfers between devices: 25.1 us -> 51.3 us  [on_device(): lax.psum_scatter(d_values, 'ctx', scatter_dimension=1, tiled=True)]
    psum x1, waiting for transfers between devices: 155 us -> 175 us  [on_device(): d_xnone = lax.psum(part_one, 'tp')]
    reduce_scatter x1, waiting for transfers between devices: 19.8 us -> 37.3 us  [on_device(): lax.psum_scatter(grad_gate, 'fsdp', scatter_dimension=0, tiled=True)]
  transfers between devices with their start and end apart: 21 -> 20, of which waited for: 20 -> 18; matrix products, arithmetic and copies ran while one was open for 7% -> 6% of each run, Pallas kernels for 0% -> 0%
where the time goes in v1:
time: 1260 us; the launch traced here: 1250 us
  waiting for transfers between devices  988 us (78%)
  matrix products  100 us (8%)
  blocking collectives  54.4 us (4%)
  other arithmetic  44.4 us (4%)
  local copies, waits for them, and re-layouts  32.7 us (3%)
  between operations  20.1 us (2%)
    psum x1, waiting for transfers between devices, on_device(): d_xnone = lax.psum(part_one, 'tp')  175 us
    psum x1, waiting for transfers between devices, on_device(): lax.psum(jnp.dot(attended, w_outp, preferred_element_type=jnp.float32), '...  159 us
    psum x1, waiting for transfers between devices, on_device(): d_xntwo = lax.psum(part_two, 'tp')  156 us
    psum x1, waiting for transfers between devices, on_device(): lax.psum(jnp.dot(hidden, w_downp, preferred_element_type=jnp.float32).ast...  76.2 us
    psum x1, waiting for transfers between devices, on_device(): s_lat = lax.psum(lax.psum(s_lat, 'tp'), 'ctx')  68.8 us
    reduce_scatter x1, waiting for transfers between devices, on_device(): lax.psum_scatter(d_values, 'ctx', scatter_dimension=1, tiled=True)  51.3 us
    reduce_scatter x1, waiting for transfers between devices, on_device(): lax.psum_scatter(grad_up, 'fsdp', scatter_dimension=0, tiled=True)  39.1 us
    reduce_scatter x1, waiting for transfers between devices, on_device(): lax.psum_scatter(grad_down, 'fsdp', scatter_dimension=1, tiled=True)  38.8 us
  transfers between devices with their start and end apart: 20, of which 18 were waited for; matrix products, arithmetic and copies ran while one was open for 6% of the time, Pallas kernels for 0%

profile of v1, /device:TPU:0, one launch (start us, length us, event | category | flops | bytes accessed | tf_op | source)
XLA Modules:
  0.0 1248.3 jit_solution(5815373919866852711)
XLA Ops:
  8.0 2.1 fusion.143
  10.8 6.0 all-gather
  17.5 4.3 all_gather.36
  25.2 7.9 all_gather.42
  33.1 7.5 all_gather.43
  42.5 3.3 convolution_convert_fusion.5
  45.9 5.4 all_gather.41
  53.9 5.4 all_gather.40
  60.2 7.7 all-gather.10.cloned.1.call-done
  69.7 2.4 while.100
  73.7 3.2 while.101
  74.1 2.7 fusion.301
  77.0 2.4 while.102
  79.5 3.4 while.103
  80.1 2.7 fusion.307
  82.9 2.8 fusion.153
  87.5 5.1 all-gather.1
  92.6 158.8 %all-reduce.12.cloned.1.call-done = f32[1024,1024]{1,0:T(8,128)} async-done(((f32[1024,1024]{1,0:T(8,128)}), f32[1024,1024]{1,0:T(8,128)}) %all-reduce.12.cloned.1.call-update) | async-done | bytes 4194320 | tf_op jit(solution)/shard_map/psum | solution.py:153
  251.4 3.5 multiply_reduce_fusion.2
  254.9 2.0 copy-done.2
  258.6 12.4 all-gather.12.cloned.1.call-done
  271.0 5.3 fusion.175
  276.3 15.3 %all-gather.14.cloned.1.call-done = bf16[1024,704]{0,1:T(8,128)(2,1)} async-done(((bf16[256,704]{0,1:T(8,128)(2,1)}), bf16[1024,704]{0,1:T(8,128)(2,1)}) %all-gather.14.cloned.1.call-update) | async-done | bytes 1441808 | tf_op jit(solution)/shard_map/all_gather | solution.py:61
  291.6 5.4 fusion.176
  297.0 15.3 %all-gather.16.cloned.1.call-done = bf16[704,1024]{1,0:T(8,128)(2,1)} async-done(((bf16[704,256]{1,0:T(8,128)(2,1)}), bf16[704,1024]{1,0:T(8,128)(2,1)}) %all-gather.16.cloned.1.call-update) | async-done | bytes 1441808 | tf_op jit(solution)/shard_map/all_gather | solution.py:62
  312.2 8.1 multiply_convert_fusion.1
  321.6 3.2 convolution_convert_fusion
  325.2 3.8 fusion.177
  329.1 3.9 convolution_add_fusion.1
  335.2 76.2 %all-reduce.14.cloned.1.call-done = bf16[1024,1024]{1,0:T(8,128)(2,1)} async-done(((bf16[1024,1024]{1,0:T(8,128)(2,1)}), bf16[1024,1024]{1,0:T(8,128)(2,1)}) %all-reduce.14.cloned.1.call-update) | async-done | bytes 2097168 | tf_op jit(solution)/shard_map/psum | solution.py:163
  411.4 156.3 %all-reduce.16.cloned.1.call-done = f32[1024,1024]{1,0:T(8,128)} async-done(((f32[1024,1024]{1,0:T(8,128)}), f32[1024,1024]{1,0:T(8,128)}) %all-reduce.16.cloned.1.call-update) | async-done | bytes 4194320 | tf_op jit(solution)/shard_map/psum | solution.py:189
  567.8 8.5 fusion.129
  581.4 2.8 while.104
  586.1 9.7 while.105
  591.7 2.3 fusion.328
  595.8 2.8 while.106
  600.9 10.0 while.107
  606.8 2.3 fusion.349
  611.0 3.2 pad_maximum_fusion.1
  614.2 2.8 pad_maximum_fusion
  617.3 51.3 %reduce-scatter.13.cloned.1.call-done = f32[2,512,256]{1,2,0:T(8,128)} async-done(((f32[2,1024,256]{1,2,0:T(8,128)}), f32[2,512,256]{1,2,0:T(8,128)}) %reduce-scatter.13.cloned.1.call-update) | async-done | bytes 1048592 | tf_op jit(solution)/shard_map/reduce_scatter | solution.py:289
  670.9 31.7 %reduce-scatter.11.cloned.1.call-done = f32[2,512,256]{1,2,0:T(8,128)} async-done(((f32[2,1024,256]{1,2,0:T(8,128)}), f32[2,512,256]{1,2,0:T(8,128)}) %reduce-scatter.11.cloned.1.call-update) | async-done | bytes 1048592 | tf_op jit(solution)/shard_map/reduce_scatter | solution.py:288
  707.8 3.4 convolution_dynamic-update-slice_fusion
  711.4 5.2 fusion.182
  716.7 5.3 fusion.183
  722.1 5.3 fusion.181
  728.2 3.4 fusion.151
  731.8 4.0 fusion.146
  740.2 4.0 convolution_add_fusion
  744.4 37.3 %reduce-scatter.25.cloned.1.call-done = f32[256,704]{0,1:T(8,128)} async-done(((f32[1024,704]{0,1:T(8,128)}), f32[256,704]{0,1:T(8,128)}) %reduce-scatter.25.cloned.1.call-update) | async-done | bytes 720912 | tf_op jit(solution)/shard_map/reduce_scatter | solution.py:320
  781.7 39.1 %reduce-scatter.27.cloned.1.call-done = f32[256,704]{0,1:T(8,128)} async-done(((f32[1024,704]{0,1:T(8,128)}), f32[256,704]{0,1:T(8,128)}) %reduce-scatter.27.cloned.1.call-update) | async-done | bytes 720912 | tf_op jit(solution)/shard_map/reduce_scatter | solution.py:321
  820.7 38.8 %reduce-scatter.29.cloned.1.call-done = f32[704,256]{1,0:T(8,128)} async-done(((f32[704,1024]{1,0:T(8,128)}), f32[704,256]{1,0:T(8,128)}) %reduce-scatter.29.cloned.1.call-update) | async-done | bytes 720912 | tf_op jit(solution)/shard_map/reduce_scatter | solution.py:322
  859.5 27.5 %reduce-scatter.17.cloned.1.call-done = f32[256,256]{1,0:T(8,128)} async-done(((f32[1024,256]{1,0:T(8,128)}), f32[256,256]{1,0:T(8,128)}) %reduce-scatter.17.cloned.1.call-update) | async-done | bytes 262160 | tf_op jit(solution)/shard_map/reduce_scatter | solution.py:315
  887.0 27.9 %reduce-scatter.23.cloned.1.call-done = f32[256,256]{1,0:T(8,128)} async-done(((f32[256,1024]{1,0:T(8,128)}), f32[256,256]{1,0:T(8,128)}) %reduce-scatter.23.cloned.1.call-update) | async-done | bytes 262160 | tf_op jit(solution)/shard_map/reduce_scatter | solution.py:318
  914.8 23.1 %reduce-scatter.21.cloned.1.call-done = f32[64,256]{1,0:T(8,128)} async-done(((f32[256,256]{1,0:T(8,128)}), f32[64,256]{1,0:T(8,128)}) %reduce-scatter.21.cloned.1.call-update) | async-done | bytes 65552 | tf_op jit(solution)/shard_map/reduce_scatter | solution.py:317
  938.0 23.0 %reduce-scatter.19.cloned.1.call-done = f32[64,256]{1,0:T(8,128)} async-done(((f32[256,256]{1,0:T(8,128)}), f32[64,256]{1,0:T(8,128)}) %reduce-scatter.19.cloned.1.call-update) | async-done | bytes 65552 | tf_op jit(solution)/shard_map/reduce_scatter | solution.py:316
  960.9 174.9 %all-reduce.18.cloned.1.call-done = (f32[1024,1024]{1,0:T(8,128)}, f32[256,512]{1,0:T(8,128)}) async-done(((f32[1024,1024]{1,0:T(8,128)}, f32[256,512]{1,0:T(8,128)}), (f32[1024,1024]{1,0:T(8,128)}, f32[256,512]{1,0:T(8,128)})) %all-reduce.18.cloned.1.call-update) | async-done | bytes 4718608 | tf_op jit(solution)/shard_map/psum | solution.py:306
  1137.8 3.2 fusion.137
  1141.2 4.8 fusion.142
  1146.0 7.1 all-reduce.3
  1153.3 5.7 all-reduce.4
  1160.2 68.8 %all-reduce.20.cloned.1.call-done = (f32[256,512]{1,0:T(8,128)}, f32[256,256]{1,0:T(8,128)}, f32[64,256]{1,0:T(8,128)}, f32[64,256]{1,0:T(8,128)}, f32[256,256]{...) async-done(((f32[256,512]{1,0:T(8,128)}, f32[256,256]{1,0:T(8,128)}, f32[64,256]{1,0:T(8,128)}, f32[64,256]{1,0:T(8,128)}, ...) | async-done | bytes 3342352 | tf_op jit(solution)/shard_map/psum | solution.py:328
  1229.0 2.0 copy.183
  1237.2 2.0 copy.188
  (294 shorter events, 70.9 us)
Async XLA Ops:
  7.2 33.4 %copy-start.4 = (bf16[2,512,1024]{2,1,0:T(8,128)(2,1)S(1)}, bf16[2,512,1024]{2,1,0:T(8,128)(2,1)}, u32[]{:S(2)}) copy-start(bf16[2,512,1024]{2,1,0:T(8,128)(2,1)} %param.29) | copy-start | bytes 6291460
  7.2 35.3 %all-gather.8.cloned.1.call-start = ((), (), s32[]{:S(2)}) async-start(), calls=%async_computation.10 | async-start | bytes 1310720 | tf_op jit(solution)/shard_map/all_gather | solution.py:54
  7.9 60.0 %all-gather.10.cloned.1.call-start = ((), (), s32[]{:S(2)}) async-start(), calls=%async_computation.11 | async-start | bytes 1572864 | tf_op jit(solution)/shard_map/all_gather | solution.py:77
  10.1 35.7 %copy-start.39 = (f32[1,4,2,128]{3,1,2,0:T(4,128)}, f32[1,4,2,128]{3,1,2,0:T(4,128)S(1)}, u32[]{:S(2)}) copy-start(f32[1,4,2,128]{3,1,2,0:T(4,128)S(1)} %copy.94) | copy-start | bytes 12292
  16.8 29.1 %copy-start.41 = (f32[4,1,256]{2,1,0:T(1,128)}, f32[4,1,256]{2,1,0:T(1,128)S(1)}, u32[]{:S(2)}) copy-start(f32[4,1,256]{2,1,0:T(1,128)S(1)} %convert_element_type.173) | copy-start | bytes 12292
  21.9 18.7 %copy-start.47 = (f32[2,1024]{1,0:T(2,128)}, f32[2,1024]{1,0:T(2,128)S(1)}, u32[]{:S(2)}) copy-start(f32[2,1024]{1,0:T(2,128)S(1)} %convert_element_type.138) | copy-start | bytes 24580
  33.1 26.2 %copy-start.20 = (bf16[1024,256]{1,0:T(8,128)(2,1)}, bf16[1024,256]{1,0:T(8,128)(2,1)S(1)}, u32[]{:S(2)}) copy-start(bf16[1024,256]{1,0:T(8,128)(2,1)S(1)} %all_gather.42) | copy-start | bytes 1572868
  42.5 3.4 copy-start.45
  42.5 11.4 copy-start.46
  42.5 16.9 %copy-start.7 = (bf16[1024,1024]{1,0:T(8,128)(2,1)S(1)}, bf16[1024,1024]{1,0:T(8,128)(2,1)}, u32[]{:S(2)}) copy-start(bf16[1024,1024]{1,0:T(8,128)(2,1)} %fusion.136) | copy-start | bytes 6291460
  45.8 205.6 %all-reduce.12.cloned.1.call-start = ((), (), s32[]{:S(2)}) async-start(), calls=%async_computation.12 | async-start | bytes 8388608 | tf_op jit(solution)/shard_map/psum | solution.py:153
  51.3 16.6 %copy-start.22 = (bf16[256,256]{1,0:T(8,128)(2,1)}, bf16[256,256]{1,0:T(8,128)(2,1)S(1)}, u32[]{:S(2)}) copy-start(bf16[256,256]{1,0:T(8,128)(2,1)S(1)} %all_gather.41) | copy-start | bytes 393220
  59.3 12.8 %copy-start.24 = (bf16[256,256]{1,0:T(8,128)(2,1)}, bf16[256,256]{1,0:T(8,128)(2,1)S(1)}, u32[]{:S(2)}) copy-start(bf16[256,256]{1,0:T(8,128)(2,1)S(1)} %all_gather.40) | copy-start | bytes 393220
  69.7 2.4 copy-start.13
  77.0 5.9 copy-start.16
  82.9 2.8 copy-start.18
  85.7 185.3 %all-gather.12.cloned.1.call-start = ((), (), s32[]{:S(2)}) async-start(), calls=%async_computation.13 | async-start | bytes 1802240 | tf_op jit(solution)/shard_map/all_gather | solution.py:60
  86.3 205.4 %all-gather.14.cloned.1.call-start = ((), (), s32[]{:S(2)}) async-start(), calls=%async_computation.14 | async-start | bytes 1802240 | tf_op jit(solution)/shard_map/all_gather | solution.py:61
  86.9 225.4 %all-gather.16.cloned.1.call-start = ((), (), s32[]{:S(2)}) async-start(), calls=%async_computation.15 | async-start | bytes 1802240 | tf_op jit(solution)/shard_map/all_gather | solution.py:62
  87.4 324.0 %all-reduce.14.cloned.1.call-start = ((), (), s32[]{:S(2)}) async-start(), calls=%async_computation.16 | async-start | bytes 4194304 | tf_op jit(solution)/shard_map/psum | solution.py:163
  312.2 9.3 copy-start.55
  324.8 243.0 %all-reduce.16.cloned.1.call-start = ((), (), s32[]{:S(2)}) async-start(), calls=%async_computation.17 | async-start | bytes 8388608 | tf_op jit(solution)/shard_map/psum | solution.py:189
  325.2 3.8 copy-start.54
  325.2 3.8 copy-start.58
  333.0 335.7 %reduce-scatter.13.cloned.1.call-start = ((), (), s32[]{:S(2)}) async-start(), calls=%async_computation.19 | async-start | bytes 3145728 | tf_op jit(solution)/shard_map/reduce_scatter | solution.py:289
  335.1 241.1 %copy-start.52 = (f32[2]{0:T(128)}, f32[2]{0:T(128)S(1)}, u32[]{:S(2)}) copy-start(f32[2]{0:T(128)S(1)} %slice_reduce_fusion) | copy-start | bytes 28
  567.8 8.5 copy-start.3
  567.8 8.5 copy-start.6
  567.8 9.1 copy-start.21
  614.2 88.4 %reduce-scatter.11.cloned.1.call-start = ((), (), s32[]{:S(2)}) async-start(), calls=%async_computation.18 | async-start | bytes 3145728 | tf_op jit(solution)/shard_map/reduce_scatter | solution.py:288
  617.0 87.1 %copy-start.23 = (bf16[256,256]{1,0:T(8,128)(2,1)S(1)}, bf16[256,256]{1,0:T(8,128)(2,1)}, u32[]{:S(2)}) copy-start(bf16[256,256]{1,0:T(8,128)(2,1)} %copy-done.22) | copy-start | bytes 393220
  617.0 87.4 %copy-start.25 = (bf16[256,256]{1,0:T(8,128)(2,1)S(1)}, bf16[256,256]{1,0:T(8,128)(2,1)}, u32[]{:S(2)}) copy-start(bf16[256,256]{1,0:T(8,128)(2,1)} %copy-done.24) | copy-start | bytes 393220
  617.0 127.3 %reduce-scatter.15.cloned.1.call-start = ((), (), s32[]{:S(2)}) async-start(), calls=%async_computation.20 | async-start | bytes 2621440 | tf_op jit(solution)/shard_map/reduce_scatter | solution.py:314
  704.1 7.2 copy-start.10
  704.1 3.8 copy-start.8
  711.3 70.4 %reduce-scatter.25.cloned.1.call-start = ((), (), s32[]{:S(2)}) async-start(), calls=%async_computation.25 | async-start | bytes 3604480 | tf_op jit(solution)/shard_map/reduce_scatter | solution.py:320
  716.6 104.1 %reduce-scatter.27.cloned.1.call-start = ((), (), s32[]{:S(2)}) async-start(), calls=%async_computation.26 | async-start | bytes 3604480 | tf_op jit(solution)/shard_map/reduce_scatter | solution.py:321
  722.0 137.5 %reduce-scatter.29.cloned.1.call-start = ((), (), s32[]{:S(2)}) async-start(), calls=%async_computation.27 | async-start | bytes 3604480 | tf_op jit(solution)/shard_map/reduce_scatter | solution.py:322
  727.3 4.4 copy-start.17
  727.4 4.4 copy-start.19
  727.4 159.6 %reduce-scatter.17.cloned.1.call-start = ((), (), s32[]{:S(2)}) async-start(), calls=%async_computation.21 | async-start | bytes 1310720 | tf_op jit(solution)/shard_map/reduce_scatter | solution.py:315
  731.7 4.2 copy-start.9
  731.7 4.2 copy-start.12
  731.7 5.3 copy-start.11
  731.7 6.7 copy-start.27
  731.7 183.1 %reduce-scatter.23.cloned.1.call-start = ((), (), s32[]{:S(2)}) async-start(), calls=%async_computation.24 | async-start | bytes 1310720 | tf_op jit(solution)/shard_map/reduce_scatter | solution.py:318
  735.8 2.6 copy-start.29
  735.8 202.2 %reduce-scatter.21.cloned.1.call-start = ((), (), s32[]{:S(2)}) async-start(), calls=%async_computation.23 | async-start | bytes 327680 | tf_op jit(solution)/shard_map/reduce_scatter | solution.py:317
  737.0 224.0 %reduce-scatter.19.cloned.1.call-start = ((), (), s32[]{:S(2)}) async-start(), calls=%async_computation.22 | async-start | bytes 327680 | tf_op jit(solution)/shard_map/reduce_scatter | solution.py:316
  738.1 397.8 %all-reduce.18.cloned.1.call-start = ((), (), s32[]{:S(2)}) async-start(), calls=%async_computation.28 | async-start | bytes 9437184 | tf_op jit(solution)/shard_map/psum | solution.py:306
  744.2 391.7 %copy-start.57 = (u32[32]{0:T(128)S(1)}, u32[32]{0:T(128)}, u32[]{:S(2)}) copy-start(u32[32]{0:T(128)} %constant.179) | copy-start | bytes 388
  744.2 392.9 %copy-start.44 = (s32[2,512]{1,0:T(2,128)S(1)}, s32[2,512]{1,0:T(2,128)}, u32[]{:S(2)}) copy-start(s32[2,512]{1,0:T(2,128)} %param.40) | copy-start | bytes 12292
  744.2 392.9 %copy-start.53 = (f32[2]{0:T(128)S(1)}, f32[2]{0:T(128)}, u32[]{:S(2)}) copy-start(f32[2]{0:T(128)} %copy-done.52) | copy-start | bytes 28
  744.2 393.1 %copy-start.51 = (f32[1024]{0:T(1024)S(1)}, f32[1024]{0:T(1024)}, u32[]{:S(2)}) copy-start(f32[1024]{0:T(1024)} %get-tuple-element.1045) | copy-start | bytes 12292
  744.2 393.1 %copy-start.50 = (f32[1024]{0:T(1024)S(1)}, f32[1024]{0:T(1024)}, u32[]{:S(2)}) copy-start(f32[1024]{0:T(1024)} %get-tuple-element.823) | copy-start | bytes 12292
  744.2 393.1 %copy-start.49 = (f32[1024]{0:T(1024)S(1)}, f32[1024]{0:T(1024)}, u32[]{:S(2)}) copy-start(f32[1024]{0:T(1024)} %get-tuple-element.824) | copy-start | bytes 12292
  744.2 393.5 %copy-start.5 = (bf16[2,512,1024]{2,1,0:T(8,128)(2,1)S(1)}, bf16[2,512,1024]{2,1,0:T(8,128)(2,1)}, u32[]{:S(2)}) copy-start(bf16[2,512,1024]{2,1,0:T(8,128)(2,1)} %param.29) | copy-start | bytes 6291460
  744.3 393.5 %copy-start.40 = (f32[1,4,2,128]{3,1,2,0:T(4,128)S(1)}, f32[1,4,2,128]{3,1,2,0:T(4,128)}, u32[]{:S(2)}) copy-start(f32[1,4,2,128]{3,1,2,0:T(4,128)} %copy-done.39) | copy-start | bytes 12292
  744.3 393.5 %copy-start.42 = (f32[4,1,256]{2,1,0:T(1,128)S(1)}, f32[4,1,256]{2,1,0:T(1,128)}, u32[]{:S(2)}) copy-start(f32[4,1,256]{2,1,0:T(1,128)} %copy-done.41) | copy-start | bytes 12292
  744.3 484.7 %all-reduce.20.cloned.1.call-start = ((), (), s32[]{:S(2)}) async-start(), calls=%async_computation.29 | async-start | bytes 6684672 | tf_op jit(solution)/shard_map/psum | solution.py:328
  1137.7 3.4 copy-start.1
  1141.2 4.8 copy-start.48
  1229.0 10.3 copy-start.31
  1229.0 11.1 copy-start.30
  (16 other events, 21.8 us)
Sparse Core Ops, SparseCore 0:
  9.6 19.4 all-gather.7
  46.0 21.8 all-gather.9
  85.8 165.5 all-reduce.11
  252.9 18.0 all-gather.11
  272.5 19.0 all-gather.13
  293.1 19.0 all-gather.15
  324.9 86.5 all-reduce.13
  413.8 153.9 all-reduce.15
  614.3 54.2 reduce-scatter.12
  670.7 31.8 reduce-scatter.10
  711.4 31.4 reduce-scatter.14
  745.3 36.3 reduce-scatter.24
  784.4 36.3 reduce-scatter.26
  823.1 36.3 reduce-scatter.28
  862.0 24.8 reduce-scatter.16
  889.9 24.8 reduce-scatter.22
  917.9 20.0 reduce-scatter.20
  940.9 20.0 reduce-scatter.18
  963.5 172.2 all-reduce.17
  1138.6 90.3 all-reduce.19
